TPU v7x, 32 devices: a whole 2x2x4 slice. The times are simulated.
32 devices in a mesh: groups: 2 (over x), expert: 16 (over z, y, core).
Axes of the slice: x: 2, y: 2, z: 4, core: 2. Of those that a mesh axis runs over, the one named last changes fastest.
Arguments:
- hidden_states: bfloat16 [2, 512, 4096], P(None, ('groups', 'expert')), parts along dimension 1, may hold values from -6 to 6
- expert_ids: int32 [2, 512, 8], P(None, ('groups', 'expert')), parts along dimension 1, may hold values from 0 to 15, all different within a row; in each aligned block of 16 rows (0 to 15, 16 to 31, ..., all dimensions but the last counted through in order) at most 16 rows name the same one
- router_probs: float32 [2, 512, 8], P(None, ('groups', 'expert')), parts along dimension 1, may hold values from 0.05 to 1
- swap_flags: int32 [16], replicated, may hold values from 0 to 1, as said below
- w_gate: bfloat16 [16, 4096, 768], P('expert'), may hold values from -0.09375 to 0.09375
- w_up: bfloat16 [16, 4096, 768], P('expert'), may hold values from -0.09375 to 0.09375
- w_down: bfloat16 [16, 768, 4096], P('expert'), may hold values from -0.21875 to 0.21875
Outputs:
- mixed: bfloat16 [2, 512, 4096], P(None, ('groups', 'expert')), parts along dimension 1
There are 2 independent parts, one for each index of `groups`. A program takes and returns all parts, laid end to end along the dimension named above; an argument that names none is the same for every part. Nothing has to cross between parts.
Inputs may be any that keep to these rules, and one draw needn't show every extreme that they name: `expert_ids`: within one step, the 16 rows of one device (aligned blocks of 16 rows) name any one slot at most 16 times, a bound that some block reaches; the 8 ids of a row differ. swap_flags[e] equals swap_flags[e XOR 1] for every slot e.
All inputs are finite; a program needn't handle non-finite values.
Results may differ from a plain program's by a relative error of at most 0.0058.
Values may be sent and summed in bfloat16 or wider, within the bound.
A program may use at most 128 MiB of HBM per device.

v0:
```python
import jax
import jax.numpy as jnp
from jax import lax
from jax.sharding import PartitionSpec as P


def expert_mlp(rows, gate_matrix, up_matrix, down_matrix):
    gate = jnp.dot(rows, gate_matrix, preferred_element_type=jnp.float32)
    up_part = jnp.dot(rows, up_matrix, preferred_element_type=jnp.float32)
    hidden = (jax.nn.silu(gate) * up_part).astype(jnp.bfloat16)
    return jnp.dot(hidden, down_matrix, preferred_element_type=jnp.float32).astype(jnp.bfloat16)


def send_back(results):
    return lax.all_to_all(results, "expert", split_axis=0, concat_axis=0, tiled=True)


def on_device(hidden_states, expert_ids, router_probs, swap_flags, w_gate, w_up, w_down):
    devices = lax.axis_size("expert")
    owner = lax.axis_index("expert")
    step_count = hidden_states.shape[0]
    tokens_here = hidden_states.shape[1]
    model_width = hidden_states.shape[2]
    top_count = expert_ids.shape[2]
    capacity = 2 * tokens_here * top_count // devices
    experts_iota = jnp.arange(devices, dtype=jnp.int32)
    own_gate = w_gate[0]
    own_up = w_up[0]
    own_down = w_down[0]
    later_gate, later_up, later_down = (own_gate, own_up, own_down)
    outputs = []
    for step_index in range(step_count):
        states = hidden_states[step_index]
        routed = expert_ids[step_index]
        weights_raw = router_probs[step_index]
        if step_index == 0:
            gate_matrix, up_matrix, down_matrix = (own_gate, own_up, own_down)
        else:
            gate_matrix, up_matrix, down_matrix = (later_gate, later_up, later_down)
            matches = (routed[:, :, None] == experts_iota[None, None, :]).astype(jnp.int32)
            flag_of = jnp.sum(matches * swap_flags[None, None, :], axis=2)
            routed = jnp.where(flag_of == 1, jnp.bitwise_xor(routed, 1), routed)
        flat_routes = routed.reshape(-1)
        onehot = (flat_routes[:, None] == experts_iota[None, :]).astype(jnp.int32)
        before = (jnp.cumsum(onehot, axis=0) - onehot) * onehot
        slot_rank = jnp.sum(before, axis=1)
        position = flat_routes * capacity + slot_rank
        everyone, all_routes = (
            lax.all_gather(states, "expert", axis=0, tiled=True),
            lax.all_gather(routed, "expert", axis=0, tiled=True),
        )
        blocks = all_routes.reshape(devices, tokens_here * top_count)
        is_mine = (blocks == owner).astype(jnp.int32)
        rank_mine = jnp.cumsum(is_mine, axis=1) - is_mine
        source = jnp.arange(devices, dtype=jnp.int32)[:, None]
        target = jnp.where(is_mine > 0, source * capacity + rank_mine, devices * capacity).reshape(
            -1
        )
        token_row = (
            source * tokens_here
            + jnp.arange(tokens_here * top_count, dtype=jnp.int32)[None, :] // top_count
        ).reshape(-1)
        row_table = (
            jnp.full((devices * capacity,), devices * tokens_here, jnp.int32)
            .at[target]
            .set(token_row, mode="drop")
        )
        padded = jnp.concatenate([everyone, jnp.zeros((1, model_width), jnp.bfloat16)], axis=0)
        results = expert_mlp(padded[row_table], gate_matrix, up_matrix, down_matrix)
        returned = send_back(results.reshape(devices, capacity, model_width))
        picked = (
            returned.reshape(-1, model_width)[position]
            .reshape(tokens_here, top_count, model_width)
            .astype(jnp.float32)
        )
        shares = weights_raw / jnp.sum(weights_raw, axis=-1, keepdims=True)
        outputs.append(jnp.sum(shares[:, :, None] * picked, axis=1).astype(jnp.bfloat16))
    return jnp.stack(outputs)


def solution(mesh):
    return jax.shard_map(
        on_device,
        mesh=mesh,
        in_specs=(
            P(None, ("groups", "expert"), None),
            P(None, ("groups", "expert"), None),
            P(None, ("groups", "expert"), None),
            P(),
            P("expert", None, None),
            P("expert", None, None),
            P("expert", None, None),
        ),
        out_specs=P(None, ("groups", "expert"), None),
        check_vma=False,
    )
```

profile of v0, /device:TPU:13, one launch (start us, length us, event | category | flops | bytes accessed | tf_op | source)
XLA Modules:
  0.0 198.4 jit_solution(17438425062962475423)
XLA Ops:
  6.5 1.7 fusion.51
  9.8 1.1 select_reduce_fusion.1
  10.9 15.8 %all-gather.3 = s32[16,16,8]{1,2,0:T(8,128)S(1)} all-gather(s32[1,16,8]{1,2,0:T(8,128)S(1)} %bitcast.96), channel_id=1, replica_groups=mesh['groups'=2,'expert'=16] {'expert'}, dimensions={0}, use_global_device_ids=true | all-gather | bytes 8704 | tf_op jit(solution)/shard_map/all_gather | solution.py:50
  27.2 21.9 %all-gather.1 = s32[1,256,8]{2,0,1:T(1,128)S(1)} all-gather(s32[1,16,8]{2,0,1:T(1,128)S(1)} %copy.54), channel_id=3, replica_groups=mesh['groups'=2,'expert'=16] {'expert'}, dimensions={1}, use_global_device_ids=true | all-gather | bytes 8704 | tf_op jit(solution)/shard_map/all_gather | solution.py:50
  49.9 1.0 fusion.50
  51.6 8.0 %scatter_custom_fusion.1 = s32[256]{0:T(256)S(1)} fusion(s32[2048]{0:T(1024)S(1)} %bitcast.98, s32[2048]{0:T(1024)S(1)} %add_bitcast_fusion, s32[]{:T(128)} %constant.49.clone.1), kind=kCustom, calls=%fused_computation.75 | custom fusion | bytes 1028 | tf_op jit(solution)/shard_map/scatter | solution.py:66
  59.7 1.8 concatenate.7
  61.5 3.1 %gather_fusion.2 = bf16[256,4096]{1,0:T(8,128)(2,1)} fusion(bf16[257,4096]{1,0:T(8,128)(2,1)S(1)} %concatenate.7, s32[1024]{0:T(1024)S(1)} %pad_clamp_fusion.1), kind=kCustom, calls=%fused_computation.2 | custom fusion | bytes 4195328 | tf_op jit(solution)/shard_map/gather | solution.py:69
  64.7 5.4 %fusion.8 = f32[256,768]{1,0:T(8,128)S(1)} fusion(bf16[256,4096]{1,0:T(8,128)(2,1)} %gather_fusion.2, bf16[1,4096,768]{2,1,0:T(8,128)(2,1)} %param.11), kind=kOutput, calls=%fused_computation.14 | convolution fusion | flops 1610612736 | bytes 9175040 | tf_op jit(solution)/shard_map/dot_general | solution.py:8
  70.1 10.5 %fusion.15 = bf16[256,4096]{1,0:T(8,128)(2,1)} fusion(bf16[1,768,4096]{2,1,0:T(8,128)(2,1)} %param.13, bf16[256,4096]{1,0:T(8,128)(2,1)S(1)} %copy-done, bf16[1,4096,768]{2,1,0:T(8,128)(2,1)} %param.12, f32[256,768]{1,0:T(8,128)S(1)} %fusion.8), kind=kOutput, calls=%fused_computation.19 | convolution fusion | flops 3223453696 | bytes 17563648 | tf_op jit(solution)/shard_map/dot_general | solution.py:11
  80.6 7.3 %all-to-all-start.1 = ((bf16[16,16,4096]{2,1,0:T(8,128)(2,1)}), bf16[16,16,4096]{2,1,0:T(8,128)(2,1)}, u32[]{:S(2)}, u32[]{:S(2)}) async-start(bf16[16,16,4096]{2,1,0:T(8,128)(2,1)} %bitcast.88), calls=%async_computation.1 | async-start | bytes 4194304 | tf_op jit(solution)/shard_map/all_to_all | solution.py:15
  87.9 8.2 %scatter_custom_fusion = s32[256]{0:T(256)S(1)} fusion(s32[2048]{0:T(1024)S(1)} %bitcast.97, s32[2048]{0:T(1024)S(1)} %add_bitcast_fusion, s32[]{:T(128)} %constant.49.clone.1), kind=kCustom, calls=%fused_computation.77 | custom fusion | bytes 1028 | tf_op jit(solution)/shard_map/scatter | solution.py:66
  96.1 1.8 concatenate.6
  97.9 3.2 %gather_fusion = bf16[256,4096]{1,0:T(8,128)(2,1)} fusion(bf16[257,4096]{1,0:T(8,128)(2,1)S(1)} %concatenate.6, s32[1024]{0:T(1024)S(1)} %pad_clamp_fusion.3), kind=kCustom, calls=%fused_computation | custom fusion | bytes 4195328 | tf_op jit(solution)/shard_map/gather | solution.py:69
  101.1 5.3 %fusion.10 = f32[256,768]{1,0:T(8,128)S(1)} fusion(bf16[256,4096]{1,0:T(8,128)(2,1)} %gather_fusion, bf16[1,4096,768]{2,1,0:T(8,128)(2,1)} %param.11), kind=kOutput, calls=%fused_computation.16 | convolution fusion | flops 1610612736 | bytes 9175040 | tf_op jit(solution)/shard_map/dot_general | solution.py:8
  106.5 10.5 %fusion.12 = bf16[256,4096]{1,0:T(8,128)(2,1)} fusion(bf16[1,768,4096]{2,1,0:T(8,128)(2,1)} %param.13, bf16[256,4096]{1,0:T(8,128)(2,1)S(1)} %copy-done.1, bf16[1,4096,768]{2,1,0:T(8,128)(2,1)} %param.12, f32[256,768]{1,0:T(8,128)S(1)} %fusion.10), kind=kOutput, calls=%fused_computation.18 | convolution fusion | flops 3223453696 | bytes 17563648 | tf_op jit(solution)/shard_map/dot_general | solution.py:11
  117.0 19.9 %all-to-all-done.1 = bf16[16,16,4096]{2,1,0:T(8,128)(2,1)} async-done(((bf16[16,16,4096]{2,1,0:T(8,128)(2,1)}), bf16[16,16,4096]{2,1,0:T(8,128)(2,1)}, u32[]{:S(2)}, u32[]{:S(2)}) %all-to-all-start.1) | async-done | bytes 2097184 | tf_op jit(solution)/shard_map/all_to_all | solution.py:15
  136.9 4.5 %all-to-all-start = ((bf16[16,16,4096]{2,1,0:T(8,128)(2,1)}), bf16[16,16,4096]{2,1,0:T(8,128)(2,1)S(1)}, u32[]{:S(2)}, u32[]{:S(2)}) async-start(bf16[16,16,4096]{2,1,0:T(8,128)(2,1)} %bitcast.87), calls=%async_computation | async-start | bytes 4194304 | tf_op jit(solution)/shard_map/all_to_all | solution.py:15
  143.3 4.1 %gather_fusion.3 = bf16[128,4096]{1,0:T(8,128)(2,1)S(1)} fusion(bf16[256,4096]{1,0:T(8,128)(2,1)} %bitcast.23, s32[1024]{0:T(1024)S(1)} %pad_clamp_fusion), kind=kCustom, calls=%fused_computation.3 | custom fusion | bytes 2097664 | tf_op jit(solution)/shard_map/gather | solution.py:72
  147.4 0.8 fusion.18
  148.2 40.7 %all-to-all-done = bf16[16,16,4096]{2,1,0:T(8,128)(2,1)S(1)} async-done(((bf16[16,16,4096]{2,1,0:T(8,128)(2,1)}), bf16[16,16,4096]{2,1,0:T(8,128)(2,1)S(1)}, u32[]{:S(2)}, u32[]{:S(2)}) %all-to-all-start) | async-done | bytes 2097184 | tf_op jit(solution)/shard_map/all_to_all | solution.py:15
  188.8 1.2 gather_fusion.1
  190.0 0.8 fusion.19
  190.8 0.7 pad_maximum_fusion
  (60 shorter events, 5.4 us)
Async XLA Ops:
  6.5 53.2 %all-gather.9.cloned.1.call-start = ((), (), s32[]{:S(2)}) async-start(), calls=%async_computation.3 | async-start | bytes 2228224 | tf_op jit(solution)/shard_map/all_gather | solution.py:49
  8.2 87.9 %all-gather.7.cloned.1.call-start = ((), (), s32[]{:S(2)}) async-start(), calls=%async_computation.2 | async-start | bytes 2228224 | tf_op jit(solution)/shard_map/all_gather | solution.py:49
  64.7 5.4 %copy-start = (bf16[256,4096]{1,0:T(8,128)(2,1)S(1)}, bf16[256,4096]{1,0:T(8,128)(2,1)}, u32[]{:S(2)}) copy-start(bf16[256,4096]{1,0:T(8,128)(2,1)} %gather_fusion.2) | copy-start | bytes 6291460
  80.6 56.3 %all-to-all-start.1 = ((bf16[16,16,4096]{2,1,0:T(8,128)(2,1)}), bf16[16,16,4096]{2,1,0:T(8,128)(2,1)}, u32[]{:S(2)}, u32[]{:S(2)}) async-start(bf16[16,16,4096]{2,1,0:T(8,128)(2,1)} %bitcast.88), calls=%async_computation.1 | async-start | bytes 4194304 | tf_op jit(solution)/shard_map/all_to_all | solution.py:15
  101.1 5.4 %copy-start.1 = (bf16[256,4096]{1,0:T(8,128)(2,1)S(1)}, bf16[256,4096]{1,0:T(8,128)(2,1)}, u32[]{:S(2)}) copy-start(bf16[256,4096]{1,0:T(8,128)(2,1)} %gather_fusion) | copy-start | bytes 6291460
  136.9 5.2 %copy-start.2 = (f32[2,16,8]{1,2,0:T(8,128)S(1)}, f32[2,16,8]{1,2,0:T(8,128)}, u32[]{:S(2)}) copy-start(f32[2,16,8]{1,2,0:T(8,128)} %param.9) | copy-start | bytes 3076
  136.9 51.9 %all-to-all-start = ((bf16[16,16,4096]{2,1,0:T(8,128)(2,1)}), bf16[16,16,4096]{2,1,0:T(8,128)(2,1)S(1)}, u32[]{:S(2)}, u32[]{:S(2)}) async-start(bf16[16,16,4096]{2,1,0:T(8,128)(2,1)} %bitcast.87), calls=%async_computation | async-start | bytes 4194304 | tf_op jit(solution)/shard_map/all_to_all | solution.py:15
Sparse Core Ops, SparseCore 0:
  9.5 41.5 all-gather.8
  53.2 40.0 all-gather.6
where the time goes:
time: 199 us; the launch traced here: 198 us
  waiting for transfers between devices  61.3 us (31%)
  blocking collectives  37.7 us (19%)
  local copies, waits for them, and re-layouts  36.1 us (18%)
  matrix products  31.8 us (16%)
  between operations  13.7 us (7%)
  starting transfers between devices  11.8 us (6%)
  other arithmetic  6.04 us (3%)
    all_to_all x2, waiting for transfers between devices, send_back(): lax.all_to_all(results, 'expert', split_axis=0, concat_axis=0, tiled=True)  60.6 us
    all_gather x2, blocking collectives, on_device(): lax.all_gather(routed, 'expert', axis=0, tiled=True)  37.7 us
    dot_general x2, matrix products, expert_mlp(): jnp.dot(hidden, down_matrix, preferred_element_type=jnp.float32)  21 us
    scatter x2, local copies, waits for them, and re-layouts, on_device(): row_table = jnp.full((devices * capacity,), devices * tokens_here, jnp.in...  16.2 us
    all_to_all x2, starting transfers between devices, send_back(): lax.all_to_all(results, 'expert', split_axis=0, concat_axis=0, tiled=True)  11.8 us
    dot_general x2, matrix products, expert_mlp(): gate = jnp.dot(rows, gate_matrix, preferred_element_type=jnp.float32)  10.7 us
    gather x2, local copies, waits for them, and re-layouts, on_device(): results = expert_mlp(padded[row_table], gate_matrix, up_matrix, down_matrix)  6.35 us
    gather x2, local copies, waits for them, and re-layouts, on_device(): returned.reshape(-1, model_width)[position]  5.25 us
  transfers between devices with their start and end apart: 4, of which 2 were waited for; matrix products, arithmetic and copies ran while one was open for 35% of the time, Pallas kernels for 0%

commit v1 on v0

v1 whole, which is shorter than its diff:
```python
import functools

import jax
import jax.numpy as jnp
from jax import lax
from jax.experimental import pallas as pl
from jax.experimental.pallas import tpu as pltpu
from jax.sharding import PartitionSpec as P

MESH = pl.DeviceIdType.MESH
CHUNKS = 4
F32 = jnp.float32
BF16 = jnp.bfloat16


def moe_kernel(
    n, x_ref, coef_ref, wg_hbm, wu_hbm, wd_hbm, out_ref,
    tok, coef, wg, wu, wd, acc_g, acc_u, hid, part, r1, q, r2, w, r3,
    z_send, z_recv, y_send, y_recv, s_send, s_recv, c_send, c_recv,
    r1_send, r1_recv, r2_send, r2_recv, r3_send, r3_recv, w_sem, own_sem,
):
    nz = n // 4
    steps, rows, width = x_ref.shape
    dc = width // CHUNKS
    units = steps * CHUNKS
    me = lax.axis_index("expert")
    k = lax.rem(me, 2)
    y = lax.rem(lax.div(me, 2), 2)
    z = lax.div(me, 4)
    ok, oy = 1 - k, 1 - y

    def zat(d):
        return lax.rem(z + d + nz, nz)

    def dev(zz, yy, kk):
        return {"expert": zz * 4 + yy * 2 + kk}

    def remote(src, dst, ss, rs, target):
        return pltpu.make_async_remote_copy(
            src_ref=src, dst_ref=dst, send_sem=ss, recv_sem=rs,
            device_id=target, device_id_type=MESH,
        )

    sib = dev(z, y, ok)
    ynb = dev(z, oy, k)

    wcopies = {}
    for c in range(CHUNKS):
        part_rows = pl.ds(c * dc, dc)
        wcopies["g", c] = pltpu.make_async_copy(wg_hbm.at[0, part_rows], wg.at[part_rows], w_sem.at[0, c])
        wcopies["u", c] = pltpu.make_async_copy(wu_hbm.at[0, part_rows], wu.at[part_rows], w_sem.at[1, c])
        wcopies["d", c] = pltpu.make_async_copy(wd_hbm.at[0, :, part_rows], wd.at[:, part_rows], w_sem.at[2, c])

    barrier = pltpu.get_barrier_semaphore()
    for d in range(1, n):
        pl.semaphore_signal(
            barrier, inc=1, device_id={"expert": lax.rem(me + d, n)}, device_id_type=MESH
        )
    for name in ("g", "u"):
        wcopies[name, 0].start()
    own = pltpu.make_async_copy(x_ref, tok.at[:, k, y, z], own_sem)
    own.start()
    pl.semaphore_wait(barrier, n - 1)

    def cols(u):
        return u // CHUNKS, pl.ds((u % CHUNKS) * dc, dc)

    def xs(u):
        s, cc = cols(u)
        return x_ref.at[s, :, cc]

    def slot(u, kk, yy, zz):
        s, cc = cols(u)
        return tok.at[s, kk, yy, zz, :, cc]

    def column(u, kk, yy):
        s, cc = cols(u)
        return tok.at[s, kk, yy, :, :, cc]

    sends = []

    def send(copy):
        copy.start()
        sends.append(copy)

    def ag1(u):
        for d in range(1, nz):
            send(remote(xs(u), slot(u, k, y, z), z_send.at[u, d - 1], z_recv.at[u, d - 1], dev(zat(d), y, k)))

    def ag2(u):
        send(remote(xs(u), slot(u, k, y, z), y_send.at[u, 0], y_recv.at[u, 0], ynb))
        for d in range(1, nz):
            here = slot(u, k, y, zat(-d))
            remote(here, here, z_send.at[u, d - 1], z_recv.at[u, d - 1], sib).wait_recv()
            send(remote(here, here, y_send.at[u, d], y_recv.at[u, d], ynb))
        col = column(u, k, y)
        send(remote(col, col, s_send.at[u, 0], s_recv.at[u, 0], sib))

    def ag3(u):
        for d in range(nz):
            here = slot(u, k, oy, zat(-d))
            remote(here, here, y_send.at[u, d], y_recv.at[u, d], ynb).wait_recv()
        col = column(u, k, oy)
        send(remote(col, col, s_send.at[u, 1], s_recv.at[u, 1], sib))

    def ag4(u):
        for i, yy in enumerate((y, oy)):
            col = column(u, ok, yy)
            remote(col, col, s_send.at[u, i], s_recv.at[u, i], sib).wait_recv()

    def gate_up(u):
        s, cc = cols(u)
        c = u % CHUNKS
        if s == 0:
            wcopies["g", c].wait()
            wcopies["u", c].wait()
        lhs = tok[s, :, :, :, :, cc].reshape(n * rows, dc)
        g = jnp.dot(lhs, wg[cc, :], preferred_element_type=F32)
        up = jnp.dot(lhs, wu[cc, :], preferred_element_type=F32)
        if c > 0:
            g = acc_g[...] + g
            up = acc_u[...] + up
        if c < CHUNKS - 1:
            acc_g[...] = g
            acc_u[...] = up
        else:
            hid[...] = (g / (1.0 + jnp.exp(-g)) * up).astype(BF16)

    def share_column(s):
        table = coef[...].reshape(n, 1, 128)
        spread = jnp.broadcast_to(table, (n, rows, 128)).reshape(n * rows, 128)
        lane = lax.broadcasted_iota(jnp.int32, (n * rows, 128), 1)
        token = lax.rem(lax.broadcasted_iota(jnp.int32, (n * rows, 128), 0), rows)
        return jnp.sum(jnp.where(lane == token + s * rows, spread, 0.0), axis=1, keepdims=True)

    def down(u):
        s, cc = cols(u)
        if s == 0:
            wcopies["d", u % CHUNKS].wait()
        res = jnp.dot(hid[...], wd[:, cc], preferred_element_type=F32)
        part[u] = (res * share_column(s)).astype(BF16).reshape(2, 2, nz, rows, dc)
        send(remote(part.at[u, ok], r1.at[u], r1_send.at[u], r1_recv.at[u], sib))

    def rs2(u):
        remote(r1.at[u], r1.at[u], r1_send.at[u], r1_recv.at[u], sib).wait_recv()
        q[u] = (part[u, k, oy].astype(F32) + r1[u, oy].astype(F32)).astype(BF16)
        send(remote(q.at[u], r2.at[u], r2_send.at[u], r2_recv.at[u], ynb))

    def rs3(u):
        remote(r2.at[u], r2.at[u], r2_send.at[u], r2_recv.at[u], ynb).wait_recv()
        total = part[u, k, y].astype(F32) + r1[u, y].astype(F32) + r2[u].astype(F32)
        w[u] = total.astype(BF16)
        for d in range(1, nz):
            send(remote(w.at[u, zat(d)], r3.at[u, d - 1], r3_send.at[u, d - 1], r3_recv.at[u, d - 1], dev(zat(d), y, k)))

    def rs4(u):
        s, cc = cols(u)
        total = part[u, k, y, z].astype(F32) + r1[u, y, z].astype(F32) + r2[u, z].astype(F32)
        for d in range(1, nz):
            here = r3.at[u, d - 1]
            remote(here, here, r3_send.at[u, d - 1], r3_recv.at[u, d - 1], sib).wait_recv()
            total = total + r3[u, d - 1].astype(F32)
        out_ref[s, :, cc] = total.astype(BF16)

    ag1(0)
    place = k * (2 * nz) + y * nz + z
    for d in range(1, n):
        to = lax.rem(me + d, n)
        send(remote(coef_ref.at[to], coef.at[place], c_send.at[d - 1], c_recv.at[d - 1], {"expert": to}))
    coef[place] = coef_ref[me]
    for u in range(1, units):
        ag1(u)
    for c in range(1, CHUNKS):
        wcopies["g", c].start()
        wcopies["u", c].start()
    for c in range(CHUNKS):
        wcopies["d", c].start()
    own.wait()

    down_at = {}
    for s in range(steps):
        for c in range(CHUNKS):
            down_at[s * CHUNKS + c] = (s + 1) * CHUNKS + 1 + (c + 1 if s < steps - 1 else c)
    last = max(down_at.values()) + 3
    coef_done = False
    for t in range(last + 1):
        if t < units:
            ag2(t)
        if 0 <= t - 1 < units:
            ag3(t - 1)
        for stage, fn in ((1, rs2), (2, rs3), (3, rs4)):
            for u in range(units):
                if down_at[u] + stage == t:
                    fn(u)
        for u in range(units):
            if down_at[u] == t and u < units - CHUNKS:
                down(u)
        if 0 <= t - 2 < units:
            if not coef_done:
                coef_done = True
                for d in range(1, n):
                    src = lax.rem(me + n - d, n)
                    at = lax.rem(src, 2) * (2 * nz) + lax.rem(lax.div(src, 2), 2) * nz + lax.div(src, 4)
                    here = coef.at[at]
                    remote(here, here, c_send.at[d - 1], c_recv.at[d - 1], sib).wait_recv()
            ag4(t - 2)
            gate_up(t - 2)
        for u in range(units):
            if down_at[u] == t and u >= units - CHUNKS:
                down(u)
    for copy in sends:
        copy.wait_send()


def moe(n, x, coef, wg, wu, wd):
    steps, rows, width = x.shape
    hidden = wg.shape[2]
    nz = n // 4
    dc = width // CHUNKS
    units = steps * CHUNKS
    vm = pltpu.VMEM
    dma = pltpu.SemaphoreType.DMA
    vspec = pl.BlockSpec(memory_space=pltpu.VMEM)
    hspec = pl.BlockSpec(memory_space=pl.ANY)
    return pl.pallas_call(
        functools.partial(moe_kernel, n),
        out_shape=jax.ShapeDtypeStruct(x.shape, BF16),
        in_specs=[vspec, vspec, hspec, hspec, hspec],
        out_specs=vspec,
        scratch_shapes=[
            vm((steps, 2, 2, nz, rows, width), BF16),
            vm((n, 1, 128), F32),
            vm((width, hidden), BF16),
            vm((width, hidden), BF16),
            vm((hidden, width), BF16),
            vm((n * rows, hidden), F32),
            vm((n * rows, hidden), F32),
            vm((n * rows, hidden), BF16),
            vm((units, 2, 2, nz, rows, dc), BF16),
            vm((units, 2, nz, rows, dc), BF16),
            vm((units, nz, rows, dc), BF16),
            vm((units, nz, rows, dc), BF16),
            vm((units, nz, rows, dc), BF16),
            vm((units, nz - 1, rows, dc), BF16),
            dma((units, nz - 1)), dma((units, nz - 1)),
            dma((units, nz)), dma((units, nz)),
            dma((units, 2)), dma((units, 2)),
            dma((n - 1,)), dma((n - 1,)),
            dma((units,)), dma((units,)),
            dma((units,)), dma((units,)),
            dma((units, nz - 1)), dma((units, nz - 1)),
            dma((3, CHUNKS)), dma,
        ],
        compiler_params=pltpu.CompilerParams(
            collective_id=0, has_side_effects=True, vmem_limit_bytes=67000000
        ),
    )(x, coef, wg, wu, wd)


def on_device(hidden_states, expert_ids, router_probs, swap_flags, w_gate, w_up, w_down):
    n = lax.axis_size("expert")
    steps, rows, _ = hidden_states.shape
    shares = router_probs / jnp.sum(router_probs, axis=-1, keepdims=True)
    experts = jnp.arange(n, dtype=jnp.int32)
    later = jnp.where(swap_flags == 1, jnp.bitwise_xor(experts, 1), experts)
    step_of = jnp.arange(steps, dtype=jnp.int32)[:, None]
    served = jnp.where(step_of == 0, experts[None, :], later[None, :])
    match = expert_ids[None] == served.T[:, :, None, None]
    coef = jnp.sum(jnp.where(match, shares[None], 0.0), axis=-1).reshape(n, 1, steps * rows)
    coef = jnp.pad(coef, ((0, 0), (0, 0), (0, 128 - steps * rows)))
    return moe(n, hidden_states, coef, w_gate, w_up, w_down)


def solution(mesh):
    return jax.shard_map(
        on_device,
        mesh=mesh,
        in_specs=(
            P(None, ("groups", "expert"), None),
            P(None, ("groups", "expert"), None),
            P(None, ("groups", "expert"), None),
            P(),
            P("expert", None, None),
            P("expert", None, None),
            P("expert", None, None),
        ),
        out_specs=P(None, ("groups", "expert"), None),
        check_vma=False,
    )
```

time: 199 us -> 80.3 us (0.40)
  the two profiles are of different devices: /device:TPU:13 before, /device:TPU:0 now
where the time goes in v1:
time: 80.3 us; the launch traced here: 79.9 us
  Pallas kernels  75.2 us (94%)
  local copies, waits for them, and re-layouts  2.37 us (3%)
  other arithmetic  2.35 us (3%)
    pallas_call x1, Pallas kernels, moe(): pl.pallas_call(functools.partial(moe_kernel, n), out_shape=jax.ShapeDtype...  75.2 us
    unnamed x1, local copies, waits for them, and re-layouts  1.67 us

profile of v1, /device:TPU:0, one launch (start us, length us, event | category | flops | bytes accessed | tf_op | source)
XLA Modules:
  0.0 79.9 jit_solution(6259905771754329143)
XLA Ops:
  0.0 0.7 compare_select_fusion
  0.7 0.1 iota_select_fusion
  0.7 0.8 fusion.1
  1.5 0.8 %select_reduce_fusion = f32[16,2,16]{2,1,0:T(2,128)S(1)} fusion(f32[2,16,8]{1,2,0:T(8,128)S(1)} %fusion.1, s32[16,2]{1,0:T(8,128)S(1)} %iota_select_fusion, s32[2,16,8]{1,2,0:T(8,128)} %param.8), kind=kLoop, calls=%fused_computation | loop fusion | flops 11776 | bytes 4224 | tf_op jit(solution)/shard_map/reduce_sum | solution.py:269
  2.4 0.1 reshape.44
  2.4 0.6 pad.4.coef_ref
  3.1 75.2 %shard_map.73 = bf16[2,16,4096]{2,1,0:T(8,128)(2,1)} custom-call(bf16[2,16,4096]{2,1,0:T(8,128)(2,1)} %x_ref.1, f32[16,1,128]{2,1,0:T(1,128)} %pad.4.coef_ref, bf16[1,4096,768]{2,1,0:T(8,128)(2,1)} %wg_hbm.1, bf16[1,4096,768]{2,1,0:T(8,128)(2,1)} %wu_hbm.1, bf16[1,768,4096]{2,1,0:T(8,128)(2,1)} %wd_hbm.1), custom_call_target="tpu_custom_call" | custom-call | tf_op jit(solution)/shard_map/pallas_call | solution.py:225
  78.2 1.7 %copy.11 = bf16[2,16,4096]{2,1,0:T(8,128)(2,1)} copy(bf16[2,16,4096]{2,1,0:T(8,128)(2,1)} %shard_map.73) | data formatting | bytes 524288
  (1 shorter events, 0.0 us)

commit v2 on v1

--- a/solution.py
+++ b/solution.py
@@ -14,8 +14,8 @@
 
 
 def moe_kernel(
-    n, x_ref, coef_ref, wg_hbm, wu_hbm, wd_hbm, out_ref,
-    tok, coef, wg, wu, wd, acc_g, acc_u, hid, part, r1, q, r2, w, r3,
+    n, x_ref, ids_ref, probs_ref, flag_ref, wg_hbm, wu_hbm, wd_hbm, out_ref,
+    tok, coef_ref, coef, wg, wu, wd, acc_g, acc_u, hid, part, r1, q, r2, w, r3,
     z_send, z_recv, y_send, y_recv, s_send, s_recv, c_send, c_recv,
     r1_send, r1_recv, r2_send, r2_recv, r3_send, r3_recv, w_sem, own_sem,
 ):
@@ -60,6 +60,24 @@
         wcopies[name, 0].start()
     own = pltpu.make_async_copy(x_ref, tok.at[:, k, y, z], own_sem)
     own.start()
+
+    lane = lax.broadcasted_iota(jnp.int32, (rows, 128), 1)
+    flags = jnp.zeros((rows, 128), jnp.int32)
+    for e in range(n):
+        flags = jnp.where(lane == e, flag_ref[e], flags)
+    tables = []
+    for s in range(steps):
+        served = lane if s == 0 else jnp.where(flags == 1, jnp.bitwise_xor(lane, 1), lane)
+        ids, probs = ids_ref[s], probs_ref[s]
+        shares = probs / jnp.sum(probs, axis=1, keepdims=True)
+        table = jnp.zeros((rows, 128), F32)
+        for j in range(ids.shape[1]):
+            table = jnp.where(ids[:, j : j + 1] == served, shares[:, j : j + 1], table)
+        tables.append(table)
+    tables.append(jnp.zeros((128 - steps * rows, 128), F32))
+    flipped = jnp.transpose(jnp.concatenate(tables, axis=0))
+    for e in range(n):
+        coef_ref[e] = flipped[e : e + 1]
     pl.semaphore_wait(barrier, n - 1)
 
     def cols(u):
@@ -86,9 +104,9 @@
     def ag1(u):
         for d in range(1, nz):
             send(remote(xs(u), slot(u, k, y, z), z_send.at[u, d - 1], z_recv.at[u, d - 1], dev(zat(d), y, k)))
+        send(remote(xs(u), slot(u, k, y, z), y_send.at[u, 0], y_recv.at[u, 0], ynb))
 
     def ag2(u):
-        send(remote(xs(u), slot(u, k, y, z), y_send.at[u, 0], y_recv.at[u, 0], ynb))
         for d in range(1, nz):
             here = slot(u, k, y, zat(-d))
             remote(here, here, z_send.at[u, d - 1], z_recv.at[u, d - 1], sib).wait_recv()
@@ -141,21 +159,33 @@
         part[u] = (res * share_column(s)).astype(BF16).reshape(2, 2, nz, rows, dc)
         send(remote(part.at[u, ok], r1.at[u], r1_send.at[u], r1_recv.at[u], sib))
 
+    def y_back(u, d):
+        zz = zat(d)
+        return remote(q.at[u, zz], r2.at[u, zz], r2_send.at[u, d], r2_recv.at[u, d], ynb)
+
     def rs2(u):
         remote(r1.at[u], r1.at[u], r1_send.at[u], r1_recv.at[u], sib).wait_recv()
         q[u] = (part[u, k, oy].astype(F32) + r1[u, oy].astype(F32)).astype(BF16)
-        send(remote(q.at[u], r2.at[u], r2_send.at[u], r2_recv.at[u], ynb))
+        for d in range(1, nz):
+            send(y_back(u, d))
+
+    def rs2_own(u):
+        send(y_back(u, 0))
+
+    def column_sum(u, zz):
+        return part[u, k, y, zz].astype(F32) + r1[u, y, zz].astype(F32) + r2[u, zz].astype(F32)
 
     def rs3(u):
-        remote(r2.at[u], r2.at[u], r2_send.at[u], r2_recv.at[u], ynb).wait_recv()
-        total = part[u, k, y].astype(F32) + r1[u, y].astype(F32) + r2[u].astype(F32)
-        w[u] = total.astype(BF16)
-        for d in range(1, nz):
-            send(remote(w.at[u, zat(d)], r3.at[u, d - 1], r3_send.at[u, d - 1], r3_recv.at[u, d - 1], dev(zat(d), y, k)))
+        for d in range(1, nz):
+            zz = zat(d)
+            y_back(u, d).wait_recv()
+            w[u, zz] = column_sum(u, zz).astype(BF16)
+            send(remote(w.at[u, zz], r3.at[u, d - 1], r3_send.at[u, d - 1], r3_recv.at[u, d - 1], dev(zz, y, k)))
 
     def rs4(u):
         s, cc = cols(u)
-        total = part[u, k, y, z].astype(F32) + r1[u, y, z].astype(F32) + r2[u, z].astype(F32)
+        y_back(u, 0).wait_recv()
+        total = column_sum(u, z)
         for d in range(1, nz):
             here = r3.at[u, d - 1]
             remote(here, here, r3_send.at[u, d - 1], r3_recv.at[u, d - 1], sib).wait_recv()
@@ -168,7 +198,7 @@
         to = lax.rem(me + d, n)
         send(remote(coef_ref.at[to], coef.at[place], c_send.at[d - 1], c_recv.at[d - 1], {"expert": to}))
     coef[place] = coef_ref[me]
-    for u in range(1, units):
+    for u in range(1, 2):
         ag1(u)
     for c in range(1, CHUNKS):
         wcopies["g", c].start()
@@ -177,42 +207,63 @@
         wcopies["d", c].start()
     own.wait()
 
-    down_at = {}
-    for s in range(steps):
+    def coef_wait():
+        for d in range(1, n):
+            src = lax.rem(me + n - d, n)
+            at = lax.rem(src, 2) * (2 * nz) + lax.rem(lax.div(src, 2), 2) * nz + lax.div(src, 4)
+            here = coef.at[at]
+            remote(here, here, c_send.at[d - 1], c_recv.at[d - 1], sib).wait_recv()
+
+    after = {}
+    for s in range(steps - 1):
+        base, first = (s + 1) * CHUNKS + 1, s * CHUNKS
+        half = CHUNKS // 2
         for c in range(CHUNKS):
-            down_at[s * CHUNKS + c] = (s + 1) * CHUNKS + 1 + (c + 1 if s < steps - 1 else c)
-    last = max(down_at.values()) + 3
-    coef_done = False
-    for t in range(last + 1):
+            late = c // half
+            after.setdefault(base + late, []).append((down, first + c))
+        for c in range(CHUNKS):
+            late = c // half
+            after.setdefault(base + 1 + late, []).extend([(rs2, first + c), (rs2_own, first + c)])
+        for c in range(half):
+            after.setdefault(base + 3, []).append((rs3, first + c))
+    for t in range(units + 2):
         if t < units:
             ag2(t)
+            if t + 2 < units:
+                ag1(t + 2)
         if 0 <= t - 1 < units:
             ag3(t - 1)
-        for stage, fn in ((1, rs2), (2, rs3), (3, rs4)):
-            for u in range(units):
-                if down_at[u] + stage == t:
-                    fn(u)
-        for u in range(units):
-            if down_at[u] == t and u < units - CHUNKS:
-                down(u)
-        if 0 <= t - 2 < units:
-            if not coef_done:
-                coef_done = True
-                for d in range(1, n):
-                    src = lax.rem(me + n - d, n)
-                    at = lax.rem(src, 2) * (2 * nz) + lax.rem(lax.div(src, 2), 2) * nz + lax.div(src, 4)
-                    here = coef.at[at]
-                    remote(here, here, c_send.at[d - 1], c_recv.at[d - 1], sib).wait_recv()
+        if t == 2:
+            coef_wait()
+        if t >= 2:
             ag4(t - 2)
             gate_up(t - 2)
-        for u in range(units):
-            if down_at[u] == t and u >= units - CHUNKS:
-                down(u)
+        for fn, u in after.get(t, ()):
+            fn(u)
+    tail = units - CHUNKS
+    held_back = [u for s in range(steps - 1) for u in range(s * CHUNKS + CHUNKS // 2, (s + 1) * CHUNKS)]
+    for c in range(CHUNKS + 2):
+        if c < CHUNKS:
+            down(tail + c)
+        for u in held_back[:1]:
+            rs3(u)
+        held_back = held_back[1:]
+        if 0 <= c - 1 < CHUNKS:
+            rs2(tail + c - 1)
+        if c == CHUNKS:
+            for u in range(tail, units):
+                rs2_own(u)
+        if 0 <= c - 2 < CHUNKS:
+            rs3(tail + c - 2)
+    for u in held_back:
+        rs3(u)
+    for u in range(units):
+        rs4(u)
     for copy in sends:
         copy.wait_send()
 
 
-def moe(n, x, coef, wg, wu, wd):
+def moe(n, x, ids, probs, flags, wg, wu, wd):
     steps, rows, width = x.shape
     hidden = wg.shape[2]
     nz = n // 4
@@ -225,10 +276,11 @@
     return pl.pallas_call(
         functools.partial(moe_kernel, n),
         out_shape=jax.ShapeDtypeStruct(x.shape, BF16),
-        in_specs=[vspec, vspec, hspec, hspec, hspec],
+        in_specs=[vspec, vspec, vspec, pl.BlockSpec(memory_space=pltpu.SMEM), hspec, hspec, hspec],
         out_specs=vspec,
         scratch_shapes=[
             vm((steps, 2, 2, nz, rows, width), BF16),
+            vm((n, 1, 128), F32),
             vm((n, 1, 128), F32),
             vm((width, hidden), BF16),
             vm((width, hidden), BF16),
@@ -247,28 +299,19 @@
             dma((units, 2)), dma((units, 2)),
             dma((n - 1,)), dma((n - 1,)),
             dma((units,)), dma((units,)),
-            dma((units,)), dma((units,)),
+            dma((units, nz)), dma((units, nz)),
             dma((units, nz - 1)), dma((units, nz - 1)),
             dma((3, CHUNKS)), dma,
         ],
         compiler_params=pltpu.CompilerParams(
             collective_id=0, has_side_effects=True, vmem_limit_bytes=67000000
         ),
-    )(x, coef, wg, wu, wd)
+    )(x, ids, probs, flags, wg, wu, wd)
 
 
 def on_device(hidden_states, expert_ids, router_probs, swap_flags, w_gate, w_up, w_down):
     n = lax.axis_size("expert")
-    steps, rows, _ = hidden_states.shape
-    shares = router_probs / jnp.sum(router_probs, axis=-1, keepdims=True)
-    experts = jnp.arange(n, dtype=jnp.int32)
-    later = jnp.where(swap_flags == 1, jnp.bitwise_xor(experts, 1), experts)
-    step_of = jnp.arange(steps, dtype=jnp.int32)[:, None]
-    served = jnp.where(step_of == 0, experts[None, :], later[None, :])
-    match = expert_ids[None] == served.T[:, :, None, None]
-    coef = jnp.sum(jnp.where(match, shares[None], 0.0), axis=-1).reshape(n, 1, steps * rows)
-    coef = jnp.pad(coef, ((0, 0), (0, 0), (0, 128 - steps * rows)))
-    return moe(n, hidden_states, coef, w_gate, w_up, w_down)
+    return moe(n, hidden_states, expert_ids, router_probs, swap_flags, w_gate, w_up, w_down)
 
 
 def solution(mesh):

time: 80.3 us -> 74.8 us (0.932)
  Pallas kernels: 75.2 us -> 70.1 us
  other arithmetic: 2.35 us -> 0 us
  local copies, waits for them, and re-layouts: 2.37 us -> 4.41 us
    pallas_call x1, Pallas kernels: 75.2 us -> 70.1 us  [moe(): pl.pallas_call(functools.partial(moe_kernel, n), out_shape=jax.ShapeDtype...]
    unnamed x1 -> x3, local copies, waits for them, and re-layouts: 1.67 us -> 4.41 us
    reduce_sum x1 -> x0, other arithmetic: 0.82 us -> none  [on_device(): jnp.sum(jnp.where(match, shares[None], 0.0), axis=-1)]
where the time goes in v2:
time: 74.8 us; the launch traced here: 74.6 us
  Pallas kernels  70.1 us (94%)
  local copies, waits for them, and re-layouts  4.41 us (6%)
    pallas_call x1, Pallas kernels, moe(): pl.pallas_call(functools.partial(moe_kernel, n), out_shape=jax.ShapeDtype...  70.1 us
    unnamed x3, local copies, waits for them, and re-layouts  4.41 us

profile of v2, /device:TPU:0, one launch (start us, length us, event | category | flops | bytes accessed | tf_op | source)
XLA Modules:
  0.0 74.6 jit_solution(3354674973154858710)
XLA Ops:
  0.0 1.4 %copy.8.ids_ref = s32[2,16,8]{2,1,0:T(8,128)} copy(s32[2,16,8]{1,2,0:T(8,128)} %param.8) | data formatting | bytes 2048 | tf_op args[1]
  1.4 1.4 %copy.9.probs_ref = f32[2,16,8]{2,1,0:T(8,128)} copy(f32[2,16,8]{1,2,0:T(8,128)} %param.9) | data formatting | bytes 2048 | tf_op args[2]
  2.7 70.1 %shard_map.73 = bf16[2,16,4096]{2,1,0:T(8,128)(2,1)} custom-call(bf16[2,16,4096]{2,1,0:T(8,128)(2,1)} %x_ref.1, s32[2,16,8]{2,1,0:T(8,128)} %copy.8.ids_ref, f32[2,16,8]{2,1,0:T(8,128)} %copy.9.probs_ref, s32[16]{0:T(128)} %flag_ref.1, bf16[1,4096,768]{2,1,0:T(8,128)(2,1)} %wg_hbm.1, bf16[1,4096,768]{2,1,0:T(8,128)(2,1)} %wu_hbm.1, bf16[1,768,4096]{2,1,0:T(8,128)(2,1)} %wd_hbm.1), custom_call_target="tpu_custom_call" | custom-call | tf_op jit(solution)/shard_map/pallas_call | solution.py:276
  72.9 1.7 %copy.11 = bf16[2,16,4096]{2,1,0:T(8,128)(2,1)} copy(bf16[2,16,4096]{2,1,0:T(8,128)(2,1)} %shard_map.73) | data formatting | bytes 524288
